TPU v7x, 32 devices: a whole 2x2x4 slice. The times are simulated.
32 devices in a mesh: fsdp: 2 (over x), ctx: 4 (over z), tp: 4 (over y, core).
Axes of the slice: x: 2, y: 2, z: 4, core: 2. Of those that a mesh axis runs over, the one named last changes fastest.
Arguments:
- inputs: bfloat16 [2, 1024, 1024], P('fsdp', 'ctx'), may hold values from -6 to 6
- upstream: bfloat16 [2, 1024, 1024], P('fsdp', 'ctx'), may hold values from -6 to 6
- teacher: bfloat16 [2, 1024, 1024], P('fsdp', 'ctx'), may hold values from -8 to 8
- valid: int32 [2, 1024], P('fsdp', 'ctx'), may hold values from 0 to 1, as said below
- segment: int32 [2, 1024], P('fsdp', 'ctx'), may hold values from 0 to 7, never falling along the last dimension, each value on 1 to 512 neighbouring positions
- gain_one: float32 [1024], replicated, may hold values from 0.25 to 1.75
- query_weight: bfloat16 [1024, 1024], P('fsdp', 'tp'), may hold values from -0.1875 to 0.1875
- key_weight: bfloat16 [1024, 1024], P('fsdp', 'tp'), may hold values from -0.1875 to 0.1875
- value_weight: bfloat16 [1024, 1024], P('fsdp', 'tp'), may hold values from -0.1875 to 0.1875
- out_weight: bfloat16 [1024, 1024], P('tp', 'fsdp'), may hold values from -0.75 to 0.75
- gain_two: float32 [1024], replicated, may hold values from 0.25 to 1.75
- gate_weight: bfloat16 [1024, 2816], P('fsdp', 'tp'), may hold values from -0.1875 to 0.1875
- up_weight: bfloat16 [1024, 2816], P('fsdp', 'tp'), may hold values from -0.1875 to 0.1875
- down_weight: bfloat16 [2816, 1024], P('tp', 'fsdp'), may hold values from -0.21875 to 0.21875
Outputs:
- output: bfloat16 [2, 1024, 1024], P('fsdp', 'ctx')
- loss: float32 [2], replicated
- grad_inputs: float32 [2, 1024, 1024], P('fsdp', 'ctx')
- grad_gain_one: float32 [1024], P('fsdp')
- grad_query: float32 [1024, 1024], P('fsdp', 'tp')
- grad_key: float32 [1024, 1024], P('fsdp', 'tp')
- grad_value: float32 [1024, 1024], P('fsdp', 'tp')
- grad_out: float32 [1024, 1024], P('tp', 'fsdp')
- grad_gain_two: float32 [1024], P('fsdp')
- grad_gate: float32 [1024, 2816], P('fsdp', 'tp')
- grad_up: float32 [1024, 2816], P('fsdp', 'tp')
- grad_down: float32 [2816, 1024], P('tp', 'fsdp')
Inputs may be any that keep to these rules, and one draw needn't show every extreme that they name: `segment`: segment numbers never fall along a sequence; each document has 1 to 512 positions and one has exactly 512. The first token of every sequence is valid.
All inputs are finite; a program needn't handle non-finite values.
Results may differ from a plain program's by a relative error of at most 0.018.
Values may be sent and summed in bfloat16 or wider, within the bound.
A program may use at most 128 MiB of HBM per device.

v0:
```python
import jax
import jax.numpy as jnp
from jax import lax
from jax.sharding import PartitionSpec as P

HEAD_DIM = 64


def rms_scale(values_in, scales_in):
    return (
        values_in
        * lax.rsqrt(jnp.mean(values_in * values_in, axis=-1, keepdims=True) + 1e-05)
        * scales_in
    )


def swiglu(gate_act, up_act):
    return jax.nn.silu(gate_act) * up_act


def head_total(partial_sum):
    return lax.psum(partial_sum, "tp")


def contract(left, right, pattern):
    return jnp.einsum(pattern, left, right, preferred_element_type=jnp.float32)


def shards(
    inputs,
    upstream,
    teacher,
    valid,
    segment,
    gain_one,
    query_weight,
    key_weight,
    value_weight,
    out_weight,
    gain_two,
    gate_weight,
    up_weight,
    down_weight,
):
    seq_dev, ctx_tok, width = inputs.shape
    row_count = seq_dev * ctx_tok
    head_cols = query_weight.shape[1]
    heads_here = head_cols // HEAD_DIM
    scaling = HEAD_DIM ** (-0.5)
    full_query, full_key, full_value, full_gate, full_up = (
        lax.all_gather(query_weight, "fsdp", axis=0, tiled=True),
        lax.all_gather(key_weight, "fsdp", axis=0, tiled=True),
        lax.all_gather(value_weight, "fsdp", axis=0, tiled=True),
        lax.all_gather(gate_weight, "fsdp", axis=0, tiled=True),
        lax.all_gather(up_weight, "fsdp", axis=0, tiled=True),
    )
    full_out, full_down = (
        lax.all_gather(out_weight, "fsdp", axis=1, tiled=True),
        lax.all_gather(down_weight, "fsdp", axis=1, tiled=True),
    )
    seg_whole = lax.all_gather(segment, "ctx", axis=1, tiled=True)
    seq_len = seg_whole.shape[1]
    query_places = lax.axis_index("ctx") * ctx_tok + jnp.arange(ctx_tok, dtype=jnp.int32)
    key_places = jnp.arange(seq_len, dtype=jnp.int32)
    causal = key_places[None, :] <= query_places[:, None]
    flat_in = inputs.reshape(row_count, width).astype(jnp.float32)
    normed_one = rms_scale(flat_in, gain_one).astype(jnp.bfloat16)
    queries = jnp.dot(normed_one, full_query, preferred_element_type=jnp.float32).astype(
        jnp.bfloat16
    )
    keys_low = jnp.dot(normed_one, full_key, preferred_element_type=jnp.float32).astype(
        jnp.bfloat16
    )
    values_low = jnp.dot(normed_one, full_value, preferred_element_type=jnp.float32).astype(
        jnp.bfloat16
    )
    pairs = jnp.concatenate([keys_low, values_low], axis=1).reshape(seq_dev, ctx_tok, 2 * head_cols)
    pairs_all = lax.all_gather(pairs, "ctx", axis=1, tiled=True)
    query_heads = queries.reshape(seq_dev, ctx_tok, heads_here, HEAD_DIM)

    def scores_of(query_one, pairs_one, seg_all, seg_own):
        keys_one = pairs_one[:, :head_cols].reshape(seq_len, heads_here, HEAD_DIM)
        values_one = pairs_one[:, head_cols:].reshape(seq_len, heads_here, HEAD_DIM)
        allowed = causal & (seg_all[None, :] == seg_own[:, None])
        raw_scores = contract(query_one, keys_one, "qhd,khd->hqk") * scaling
        masked = jnp.where(allowed[None], raw_scores, -1e30)
        return (keys_one, values_one, allowed, masked)

    def attend_forward(bundle):
        query_one, pairs_one, seg_all, seg_own = bundle
        keys_one, values_one, allowed, masked = scores_of(query_one, pairs_one, seg_all, seg_own)
        top_score = jnp.max(masked, axis=-1, keepdims=True)
        exponent = jnp.where(allowed[None], jnp.exp(masked - top_score), 0.0)
        denominator = jnp.sum(exponent, axis=-1, keepdims=True)
        probs_low = (exponent / denominator).astype(jnp.bfloat16)
        mixed_one = contract(probs_low, values_one, "hqk,khd->qhd")
        return (mixed_one, top_score + jnp.log(denominator))

    mixed, log_norm = lax.map(attend_forward, (query_heads, pairs_all, seg_whole, segment))
    mixed_low = mixed.reshape(row_count, head_cols).astype(jnp.bfloat16)
    middle = flat_in + head_total(jnp.dot(mixed_low, full_out, preferred_element_type=jnp.float32))
    normed_two = rms_scale(middle, gain_two).astype(jnp.bfloat16)
    gate_low = jnp.dot(normed_two, full_gate, preferred_element_type=jnp.float32).astype(
        jnp.bfloat16
    )
    up_low = jnp.dot(normed_two, full_up, preferred_element_type=jnp.float32).astype(jnp.bfloat16)
    gate_wide = gate_low.astype(jnp.float32)
    up_wide = up_low.astype(jnp.float32)
    hidden_low = swiglu(gate_wide, up_wide).astype(jnp.bfloat16)
    result = middle + head_total(jnp.dot(hidden_low, full_down, preferred_element_type=jnp.float32))
    weighting = valid.reshape(row_count, 1).astype(jnp.float32)
    differ = result - teacher.reshape(row_count, width).astype(jnp.float32)
    per_sequence = jnp.sum((weighting * differ * differ).reshape(seq_dev, ctx_tok * width), axis=1)
    all_seqs = seq_dev * lax.axis_size("fsdp")
    own_seqs = lax.axis_index("fsdp") * seq_dev + jnp.arange(seq_dev, dtype=jnp.int32)
    placed = jnp.sum(
        jnp.where(
            own_seqs[:, None] == jnp.arange(all_seqs, dtype=jnp.int32)[None, :],
            per_sequence[:, None],
            0.0,
        ),
        axis=0,
    )
    counted, squared = lax.psum((jnp.sum(weighting), placed), ("fsdp", "ctx"))
    loss_value = squared * all_seqs / (counted * width)
    cotangent = upstream.reshape(row_count, width).astype(jnp.float32) + weighting * differ
    branch_grad = cotangent.astype(jnp.bfloat16)
    grad_down = contract(hidden_low, branch_grad, "rf,rd->fd")
    hidden_grad = contract(branch_grad, full_down, "rd,fd->rf")
    ignored, swiglu_back = jax.vjp(swiglu, gate_wide, up_wide)
    gate_grad, up_grad = swiglu_back(hidden_grad)
    gate_grad = gate_grad.astype(jnp.bfloat16)
    up_grad = up_grad.astype(jnp.bfloat16)
    grad_gate = contract(normed_two, gate_grad, "rd,rf->df")
    grad_up = contract(normed_two, up_grad, "rd,rf->df")
    norm_two_grad = head_total(
        contract(gate_grad, full_gate, "rf,df->rd") + contract(up_grad, full_up, "rf,df->rd")
    )
    ignored, norm_two_back = jax.vjp(rms_scale, middle, gain_two)
    middle_part, grad_gain_two = norm_two_back(norm_two_grad)
    middle_grad = cotangent + middle_part
    attn_grad = middle_grad.astype(jnp.bfloat16)
    grad_out = contract(mixed_low, attn_grad, "rh,rd->hd")
    mixed_grad = (
        contract(attn_grad, full_out, "rd,hd->rh")
        .astype(jnp.bfloat16)
        .reshape(seq_dev, ctx_tok, heads_here, HEAD_DIM)
    )

    def attend_backward(bundle):
        query_one, pairs_one, seg_all, seg_own, lse_one, grad_one = bundle
        keys_one, values_one, allowed, masked = scores_of(query_one, pairs_one, seg_all, seg_own)
        prob_full = jnp.where(allowed[None], jnp.exp(masked - lse_one), 0.0)
        value_grad = contract(prob_full.astype(jnp.bfloat16), grad_one, "hqk,qhd->khd")
        prob_grad = contract(grad_one, values_one, "qhd,khd->hqk")
        score_grad = (
            prob_full * (prob_grad - jnp.sum(prob_full * prob_grad, axis=-1, keepdims=True))
        ).astype(jnp.bfloat16)
        query_grad = contract(score_grad, keys_one, "hqk,khd->qhd") * scaling
        key_grad = contract(score_grad, query_one, "hqk,qhd->khd") * scaling
        return (
            query_grad,
            jnp.concatenate(
                [key_grad.reshape(seq_len, head_cols), value_grad.reshape(seq_len, head_cols)],
                axis=1,
            ),
        )

    query_grads, pair_terms = lax.map(
        attend_backward, (query_heads, pairs_all, seg_whole, segment, log_norm, mixed_grad)
    )
    pair_grads = (
        lax.psum_scatter(pair_terms, "ctx", scatter_dimension=1, tiled=True)
        .astype(jnp.bfloat16)
        .reshape(row_count, 2 * head_cols)
    )
    query_low = query_grads.reshape(row_count, head_cols).astype(jnp.bfloat16)
    key_low = pair_grads[:, :head_cols]
    value_low = pair_grads[:, head_cols:]
    grad_query = contract(normed_one, query_low, "rd,rh->dh")
    grad_key = contract(normed_one, key_low, "rd,rh->dh")
    grad_value = contract(normed_one, value_low, "rd,rh->dh")
    norm_one_grad = head_total(
        contract(query_low, full_query, "rh,dh->rd")
        + contract(key_low, full_key, "rh,dh->rd")
        + contract(value_low, full_value, "rh,dh->rd")
    )
    ignored, norm_one_back = jax.vjp(rms_scale, flat_in, gain_one)
    input_part, grad_gain_one = norm_one_back(norm_one_grad)
    grad_inputs = (middle_grad + input_part).reshape(seq_dev, ctx_tok, width)
    row_query, row_key, row_value, row_gate, row_up, row_one, row_two = (
        lax.psum_scatter(
            grad_query.astype(jnp.bfloat16), "fsdp", scatter_dimension=0, tiled=True
        ).astype(jnp.float32),
        lax.psum_scatter(
            grad_key.astype(jnp.bfloat16), "fsdp", scatter_dimension=0, tiled=True
        ).astype(jnp.float32),
        lax.psum_scatter(
            grad_value.astype(jnp.bfloat16), "fsdp", scatter_dimension=0, tiled=True
        ).astype(jnp.float32),
        lax.psum_scatter(
            grad_gate.astype(jnp.bfloat16), "fsdp", scatter_dimension=0, tiled=True
        ).astype(jnp.float32),
        lax.psum_scatter(
            grad_up.astype(jnp.bfloat16), "fsdp", scatter_dimension=0, tiled=True
        ).astype(jnp.float32),
        lax.psum_scatter(
            grad_gain_one.astype(jnp.bfloat16), "fsdp", scatter_dimension=0, tiled=True
        ).astype(jnp.float32),
        lax.psum_scatter(
            grad_gain_two.astype(jnp.bfloat16), "fsdp", scatter_dimension=0, tiled=True
        ).astype(jnp.float32),
    )
    col_out, col_down = (
        lax.psum_scatter(
            grad_out.astype(jnp.bfloat16), "fsdp", scatter_dimension=1, tiled=True
        ).astype(jnp.float32),
        lax.psum_scatter(
            grad_down.astype(jnp.bfloat16), "fsdp", scatter_dimension=1, tiled=True
        ).astype(jnp.float32),
    )
    sum_query, sum_key, sum_value, sum_gate, sum_up, sum_one, sum_two, sum_out, sum_down = (
        lax.psum(row_query.astype(jnp.bfloat16), "ctx").astype(jnp.float32),
        lax.psum(row_key.astype(jnp.bfloat16), "ctx").astype(jnp.float32),
        lax.psum(row_value.astype(jnp.bfloat16), "ctx").astype(jnp.float32),
        lax.psum(row_gate.astype(jnp.bfloat16), "ctx").astype(jnp.float32),
        lax.psum(row_up.astype(jnp.bfloat16), "ctx").astype(jnp.float32),
        lax.psum(row_one.astype(jnp.bfloat16), "ctx").astype(jnp.float32),
        lax.psum(row_two.astype(jnp.bfloat16), "ctx").astype(jnp.float32),
        lax.psum(col_out.astype(jnp.bfloat16), "ctx").astype(jnp.float32),
        lax.psum(col_down.astype(jnp.bfloat16), "ctx").astype(jnp.float32),
    )
    output = result.astype(jnp.bfloat16).reshape(seq_dev, ctx_tok, width)
    return (
        output,
        loss_value,
        grad_inputs,
        sum_one,
        sum_query,
        sum_key,
        sum_value,
        sum_out,
        sum_two,
        sum_gate,
        sum_up,
        sum_down,
    )


def solution(mesh):
    placed = (
        P("fsdp", "ctx", None),
        P("fsdp", "ctx", None),
        P("fsdp", "ctx", None),
        P("fsdp", "ctx"),
        P("fsdp", "ctx"),
        P(),
        P("fsdp", "tp"),
        P("fsdp", "tp"),
        P("fsdp", "tp"),
        P("tp", "fsdp"),
        P(),
        P("fsdp", "tp"),
        P("fsdp", "tp"),
        P("tp", "fsdp"),
    )
    return jax.shard_map(
        shards,
        mesh=mesh,
        in_specs=placed,
        out_specs=(
            P("fsdp", "ctx", None),
            P(),
            P("fsdp", "ctx", None),
            P("fsdp"),
            P("fsdp", "tp"),
            P("fsdp", "tp"),
            P("fsdp", "tp"),
            P("tp", "fsdp"),
            P("fsdp"),
            P("fsdp", "tp"),
            P("fsdp", "tp"),
            P("tp", "fsdp"),
        ),
        check_vma=False,
    )
```

profile of v0, /device:TPU:0, one launch (start us, length us, event | category | flops | bytes accessed | tf_op | source)
XLA Modules:
  0.0 628.7 jit_solution(3718089470991618106)
XLA Ops:
  9.4 10.2 %all_gather.29 = bf16[1024,256]{1,0:T(8,128)(2,1)S(1)} all-gather(bf16[512,256]{1,0:T(8,128)(2,1)} %param.21), channel_id=1, replica_groups=mesh['fsdp'=2,'ctx'=4,'tp'=4] {'fsdp'}, dimensions={0}, use_global_device_ids=true | all-gather | bytes 786432 | tf_op jit(solution)/shard_map/all_gather | solution.py:52
  19.6 8.3 %all_gather.30 = bf16[1024,256]{1,0:T(8,128)(2,1)S(1)} all-gather(bf16[512,256]{1,0:T(8,128)(2,1)} %param.22), channel_id=1, replica_groups=mesh['fsdp'=2,'ctx'=4,'tp'=4] {'fsdp'}, dimensions={0}, use_global_device_ids=true | all-gather | bytes 786432 | tf_op jit(solution)/shard_map/all_gather | solution.py:53
  28.0 1.7 convolution_convert_fusion.12
  32.0 11.1 %all_gather.32 = s32[1,1024]{1,0:T(1,128)S(1)} all-gather(s32[1,256]{1,0:T(1,128)S(1)} %copy-done.47), channel_id=1, replica_groups=mesh['fsdp'=2,'ctx'=4,'tp'=4] {'ctx'}, dimensions={1}, use_global_device_ids=true | all-gather | bytes 5120 | tf_op jit(solution)/shard_map/all_gather | solution.py:61
  43.1 8.5 %all_gather.34 = bf16[1024,256]{1,0:T(8,128)(2,1)S(1)} all-gather(bf16[512,256]{1,0:T(8,128)(2,1)S(1)} %copy-done.34), channel_id=1, replica_groups=mesh['fsdp'=2,'ctx'=4,'tp'=4] {'fsdp'}, dimensions={0}, use_global_device_ids=true | all-gather | bytes 786432 | tf_op jit(solution)/shard_map/all_gather | solution.py:51
  51.5 7.0 %all_gather.35 = bf16[256,1024]{1,0:T(8,128)(2,1)S(1)} all-gather(bf16[256,512]{1,0:T(8,128)(2,1)S(1)} %copy-done.35), channel_id=1, replica_groups=mesh['fsdp'=2,'ctx'=4,'tp'=4] {'fsdp'}, dimensions={1}, use_global_device_ids=true | all-gather | bytes 786432 | tf_op jit(solution)/shard_map/all_gather | solution.py:58
  59.4 3.8 all-gather.12.cloned.1.call-done
  66.2 1.5 fusion
  68.3 1.8 fusion.15
  73.9 33.0 %all-reduce.12.cloned.1.call-done = f32[256,1024]{1,0:T(8,128)} async-done(((f32[256,1024]{1,0:T(8,128)}), f32[256,1024]{1,0:T(8,128)}) %all-reduce.12.cloned.1.call-update) | async-done | bytes 1048592 | tf_op jit(solution)/shard_map/psum | solution.py:22
  108.5 3.0 fusion.13
  111.5 13.5 %all-gather.8.cloned.1.call-done = bf16[1024,704]{0,1:T(8,128)(2,1)} async-done(((bf16[512,704]{0,1:T(8,128)(2,1)}), bf16[1024,704]{0,1:T(8,128)(2,1)}) %all-gather.8.cloned.1.call-update) | async-done | bytes 1441808 | tf_op jit(solution)/shard_map/all_gather | solution.py:55
  125.0 3.0 multiply_convert_fusion.3
  128.0 24.0 %all-gather.10.cloned.1.call-done = bf16[704,1024]{1,0:T(8,128)(2,1)} async-done(((bf16[704,512]{1,0:T(8,128)(2,1)}), bf16[704,1024]{1,0:T(8,128)(2,1)}) %all-gather.10.cloned.1.call-update) | async-done | bytes 1441808 | tf_op jit(solution)/shard_map/all_gather | solution.py:59
  152.0 2.9 fusion.60
  155.1 36.4 %all-reduce.14.cloned.1.call-done = f32[256,1024]{1,0:T(8,128)} async-done(((f32[256,1024]{1,0:T(8,128)}), f32[256,1024]{1,0:T(8,128)}) %all-reduce.14.cloned.1.call-update) | async-done | bytes 1048592 | tf_op jit(solution)/shard_map/psum | solution.py:22
  191.4 1.8 multiply_add_fusion
  193.5 2.3 multiply_convert_fusion.2
  196.7 1.6 convolution_add_fusion.2
  199.2 36.0 %all-reduce.16.cloned.1.call-done = f32[256,1024]{1,0:T(8,128)} async-done(((f32[256,1024]{1,0:T(8,128)}), f32[256,1024]{1,0:T(8,128)}) %all-reduce.16.cloned.1.call-update) | async-done | bytes 1048592 | tf_op jit(solution)/shard_map/psum | solution.py:22
  235.2 3.4 multiply_reduce_fusion.1
  242.5 1.9 multiply_reduce_fusion
  247.9 2.1 convolution_convert_fusion.3
  250.0 1.8 fusion.14
  252.5 2.3 convolution_convert_fusion.6
  254.9 2.9 convolution_convert_fusion.2
  257.9 1.6 convolution_convert_fusion
  259.6 1.6 convolution_convert_fusion.1
  261.4 30.8 %reduce-scatter.9.cloned.1.call-done = f32[1,256,512]{1,2,0:T(8,128)} async-done(((f32[1,1024,512]{1,2,0:T(8,128)}), f32[1,256,512]{1,2,0:T(8,128)}) %reduce-scatter.9.cloned.1.call-update) | async-done | bytes 524304 | tf_op jit(solution)/shard_map/reduce_scatter | solution.py:173
  298.0 10.0 %reduce-scatter.17.cloned.1.call-done = bf16[256,512]{1,0:T(8,128)(2,1)} async-done(((bf16[256,1024]{1,0:T(8,128)(2,1)}), bf16[256,512]{1,0:T(8,128)(2,1)}) %reduce-scatter.17.cloned.1.call-update) | async-done | bytes 262160 | tf_op jit(solution)/shard_map/reduce_scatter | solution.py:215
  308.1 17.5 %reduce-scatter.11.cloned.1.call-done = bf16[512,256]{1,0:T(8,128)(2,1)} async-done(((bf16[1024,256]{1,0:T(8,128)(2,1)}), bf16[512,256]{1,0:T(8,128)(2,1)}) %reduce-scatter.11.cloned.1.call-update) | async-done | bytes 262160 | tf_op jit(solution)/shard_map/reduce_scatter | solution.py:192
  325.6 27.6 %reduce-scatter.23.cloned.1.call-done = bf16[704,512]{1,0:T(8,128)(2,1)} async-done(((bf16[704,1024]{1,0:T(8,128)(2,1)}), bf16[704,512]{1,0:T(8,128)(2,1)}) %reduce-scatter.23.cloned.1.call-update) | async-done | bytes 720912 | tf_op jit(solution)/shard_map/reduce_scatter | solution.py:218
  353.1 27.6 %reduce-scatter.21.cloned.1.call-done = bf16[512,704]{0,1:T(8,128)(2,1)} async-done(((bf16[1024,704]{0,1:T(8,128)(2,1)}), bf16[512,704]{0,1:T(8,128)(2,1)}) %reduce-scatter.21.cloned.1.call-update) | async-done | bytes 720912 | tf_op jit(solution)/shard_map/reduce_scatter | solution.py:204
  380.7 27.4 %reduce-scatter.19.cloned.1.call-done = bf16[512,704]{0,1:T(8,128)(2,1)} async-done(((bf16[1024,704]{0,1:T(8,128)(2,1)}), bf16[512,704]{0,1:T(8,128)(2,1)}) %reduce-scatter.19.cloned.1.call-update) | async-done | bytes 720912 | tf_op jit(solution)/shard_map/reduce_scatter | solution.py:201
  408.1 17.5 %reduce-scatter.13.cloned.1.call-done = bf16[512,256]{1,0:T(8,128)(2,1)} async-done(((bf16[1024,256]{1,0:T(8,128)(2,1)}), bf16[512,256]{1,0:T(8,128)(2,1)}) %reduce-scatter.13.cloned.1.call-update) | async-done | bytes 262160 | tf_op jit(solution)/shard_map/reduce_scatter | solution.py:195
  425.6 17.3 %reduce-scatter.15.cloned.1.call-done = bf16[512,256]{1,0:T(8,128)(2,1)} async-done(((bf16[1024,256]{1,0:T(8,128)(2,1)}), bf16[512,256]{1,0:T(8,128)(2,1)}) %reduce-scatter.15.cloned.1.call-update) | async-done | bytes 262160 | tf_op jit(solution)/shard_map/reduce_scatter | solution.py:198
  445.5 21.2 %all-reduce.2 = (f32[2]{0:T(128)S(1)}, f32[]{:T(128)}) all-reduce(f32[2]{0:T(128)S(1)} %compare_select_fusion, f32[]{:T(128)} %convert_reduce_fusion), channel_id=1, replica_groups=mesh['fsdp'=2,'ctx'=4,'tp'=4] {'fsdp','ctx'}, use_global_device_ids=true, to_apply=%region_7.8 | all-reduce | flops 3 | bytes 24 | tf_op jit(solution)/shard_map/psum | solution.py:124
  467.8 14.4 %all-reduce.18.cloned.1.call-done = f32[256,1024]{1,0:T(8,128)} async-done(((f32[256,1024]{1,0:T(8,128)}), f32[256,1024]{1,0:T(8,128)}) %all-reduce.18.cloned.1.call-update) | async-done | bytes 1048592 | tf_op jit(solution)/shard_map/psum | solution.py:22
  482.2 1.6 fusion.17
  483.8 4.9 all-reduce.5
  488.9 12.3 %all-reduce.3 = (bf16[512]{0:T(512)(128)(2,1)S(1)}, bf16[512]{0:T(512)(128)(2,1)S(1)}) all-reduce(bf16[512]{0:T(512)(128)(2,1)S(1)} %dynamic-slice.2, bf16[512]{0:T(512)(128)(2,1)S(1)} %dynamic-slice.4), channel_id=1, replica_groups=mesh['fsdp'=2,'ctx'=4,'tp'=4] {'ctx'}, use_global_device_ids=true, to_apply=%region_18.19 | all-reduce | flops 1024 | bytes 4096 | tf_op jit(solution)/shard_map/psum | solution.py:228
  502.3 2.5 fusion.25
  504.8 104.2 %all-reduce.20.cloned.1.call-done = (bf16[512,256]{1,0:T(8,128)(2,1)}, bf16[512,256]{1,0:T(8,128)(2,1)}, bf16[512,256]{1,0:T(8,128)(2,1)}, bf16[256,512]{1,0:T(8...) async-done(((bf16[512,256]{1,0:T(8,128)(2,1)}, bf16[512,256]{1,0:T(8,128)(2,1)}, bf16[512,256]{1,0:T(8,128)(2,1)}, ...) | async-done | bytes 3211280 | tf_op jit(solution)/shard_map/psum | solution.py:223
  609.1 1.9 convert_element_type.237
  610.9 1.8 convert_element_type.239
  612.7 1.8 convert_element_type.241
  614.5 1.8 convert_element_type.243
  616.3 2.4 convert_element_type.247
  (179 shorter events, 35.8 us)
Async XLA Ops:
  8.0 50.9 %copy-start.3 = (bf16[1,256,1024]{2,1,0:T(8,128)(2,1)S(1)}, bf16[1,256,1024]{2,1,0:T(8,128)(2,1)}, u32[]{:S(2)}) copy-start(bf16[1,256,1024]{2,1,0:T(8,128)(2,1)} %param.14) | copy-start | bytes 1572868
  8.0 50.9 %copy-start.37 = (f32[1024]{0:T(1024)S(1)}, f32[1024]{0:T(1024)}, u32[]{:S(2)}) copy-start(f32[1024]{0:T(1024)} %param.19) | copy-start | bytes 12292
  8.0 23.9 %copy-start.47 = (s32[1,256]{1,0:T(1,128)S(1)}, s32[1,256]{1,0:T(1,128)}, u32[]{:S(2)}) copy-start(s32[1,256]{1,0:T(1,128)} %param.18) | copy-start | bytes 3076
  8.0 35.0 %copy-start.34 = (bf16[512,256]{1,0:T(8,128)(2,1)S(1)}, bf16[512,256]{1,0:T(8,128)(2,1)}, u32[]{:S(2)}) copy-start(bf16[512,256]{1,0:T(8,128)(2,1)} %param.20) | copy-start | bytes 786436
  8.1 43.5 %copy-start.35 = (bf16[256,512]{1,0:T(8,128)(2,1)S(1)}, bf16[256,512]{1,0:T(8,128)(2,1)}, u32[]{:S(2)}) copy-start(bf16[256,512]{1,0:T(8,128)(2,1)} %param.23) | copy-start | bytes 786436
  8.1 55.1 %all-gather.12.cloned.1.call-start = ((), (), s32[]{:S(2)}) async-start(), calls=%async_computation.23 | async-start | bytes 1310720 | tf_op jit(solution)/shard_map/all_gather | solution.py:78
  9.4 22.6 %copy-start.41 = (f32[256]{0:T(256)}, f32[256]{0:T(256)S(1)}, u32[]{:S(2)}) copy-start(f32[256]{0:T(256)S(1)} %fusion.18) | copy-start | bytes 3076
  9.4 49.9 %copy-start.44 = (f32[256]{0:T(256)}, f32[256]{0:T(256)S(1)}, u32[]{:S(2)}) copy-start(f32[256]{0:T(256)S(1)} %fusion.44) | copy-start | bytes 3076
  19.6 8.3 %copy-start.17 = (bf16[1024,256]{1,0:T(8,128)(2,1)}, bf16[1024,256]{1,0:T(8,128)(2,1)S(1)}, u32[]{:S(2)}) copy-start(bf16[1024,256]{1,0:T(8,128)(2,1)S(1)} %all_gather.29) | copy-start | bytes 1572868
  28.0 15.1 %copy-start.15 = (bf16[1024,256]{1,0:T(8,128)(2,1)}, bf16[1024,256]{1,0:T(8,128)(2,1)S(1)}, u32[]{:S(2)}) copy-start(bf16[1024,256]{1,0:T(8,128)(2,1)S(1)} %all_gather.30) | copy-start | bytes 1572868
  31.9 74.9 %all-reduce.12.cloned.1.call-start = ((), (), s32[]{:S(2)}) async-start(), calls=%async_computation.8 | async-start | bytes 2097152 | tf_op jit(solution)/shard_map/psum | solution.py:22
  51.5 7.3 %copy-start.13 = (bf16[1024,256]{1,0:T(8,128)(2,1)}, bf16[1024,256]{1,0:T(8,128)(2,1)S(1)}, u32[]{:S(2)}) copy-start(bf16[1024,256]{1,0:T(8,128)(2,1)S(1)} %all_gather.34) | copy-start | bytes 1572868
  58.6 11.5 %copy-start.8 = (bf16[256,1024]{1,0:T(8,128)(2,1)}, bf16[256,1024]{1,0:T(8,128)(2,1)S(1)}, u32[]{:S(2)}) copy-start(bf16[256,1024]{1,0:T(8,128)(2,1)S(1)} %all_gather.35) | copy-start | bytes 1572868
  70.1 38.2 %copy-start.36 = (f32[1024]{0:T(1024)S(1)}, f32[1024]{0:T(1024)}, u32[]{:S(2)}) copy-start(f32[1024]{0:T(1024)} %param.24) | copy-start | bytes 12292
  72.1 36.5 %all-gather.6.cloned.1.call-start = ((), (), s32[]{:S(2)}) async-start(), calls=%async_computation.9 | async-start | bytes 2162688 | tf_op jit(solution)/shard_map/all_gather | solution.py:54
  72.6 52.4 %all-gather.8.cloned.1.call-start = ((), (), s32[]{:S(2)}) async-start(), calls=%async_computation.10 | async-start | bytes 2162688 | tf_op jit(solution)/shard_map/all_gather | solution.py:55
  73.2 78.8 %all-gather.10.cloned.1.call-start = ((), (), s32[]{:S(2)}) async-start(), calls=%async_computation.11 | async-start | bytes 2162688 | tf_op jit(solution)/shard_map/all_gather | solution.py:59
  73.8 117.6 %all-reduce.14.cloned.1.call-start = ((), (), s32[]{:S(2)}) async-start(), calls=%async_computation.12 | async-start | bytes 2097152 | tf_op jit(solution)/shard_map/psum | solution.py:22
  108.3 19.7 %copy-start.43 = (f32[256]{0:T(256)}, f32[256]{0:T(256)S(1)}, u32[]{:S(2)}) copy-start(f32[256]{0:T(256)S(1)} %get-tuple-element.84) | copy-start | bytes 3076
  108.5 46.5 %copy-start.5 = (bf16[256,1024]{1,0:T(8,128)(2,1)}, bf16[256,1024]{1,0:T(8,128)(2,1)S(1)}, u32[]{:S(2)}) copy-start(bf16[256,1024]{1,0:T(8,128)(2,1)S(1)} %multiply_convert_fusion.1) | copy-start | bytes 1572868
  111.5 43.5 %copy-start.48 = (s32[1,256]{1,0:T(1,128)S(1)}, s32[1,256]{1,0:T(1,128)}, u32[]{:S(2)}) copy-start(s32[1,256]{1,0:T(1,128)} %param.17) | copy-start | bytes 3076
  111.5 79.9 %copy-start.12 = (bf16[1,256,1024]{2,1,0:T(8,128)(2,1)S(1)}, bf16[1,256,1024]{2,1,0:T(8,128)(2,1)}, u32[]{:S(2)}) copy-start(bf16[1,256,1024]{2,1,0:T(8,128)(2,1)} %param.16) | copy-start | bytes 1572868
  128.0 63.5 %copy-start.23 = (bf16[256,704]{0,1:T(8,128)(2,1)}, bf16[256,704]{0,1:T(8,128)(2,1)S(1)}, u32[]{:S(2)}) copy-start(bf16[256,704]{0,1:T(8,128)(2,1)S(1)} %get-tuple-element.93) | copy-start | bytes 1081348
  155.0 80.2 %all-reduce.16.cloned.1.call-start = ((), (), s32[]{:S(2)}) async-start(), calls=%async_computation.13 | async-start | bytes 2097152 | tf_op jit(solution)/shard_map/psum | solution.py:22
  155.1 40.8 %copy-start.40 = (f32[1,256]{1,0:T(1,128)}, f32[1,256]{1,0:T(1,128)S(1)}, u32[]{:S(2)}) copy-start(f32[1,256]{1,0:T(1,128)S(1)} %convert_element_type.214) | copy-start | bytes 3076
  193.2 46.0 %copy-start.2 = (f32[256,1024]{1,0:T(8,128)}, f32[256,1024]{1,0:T(8,128)S(1)}, u32[]{:S(2)}) copy-start(f32[256,1024]{1,0:T(8,128)S(1)} %multiply_add_fusion) | copy-start | bytes 3145732
  195.8 39.3 %copy-start.11 = (f32[256,1024]{1,0:T(8,128)S(1)}, f32[256,1024]{1,0:T(8,128)}, u32[]{:S(2)}) copy-start(f32[256,1024]{1,0:T(8,128)} %all-reduce.14.cloned.1.call-done) | copy-start | bytes 3145732
  198.3 93.8 %reduce-scatter.9.cloned.1.call-start = ((), (), s32[]{:S(2)}) async-start(), calls=%async_computation.14 | async-start | bytes 2621440 | tf_op jit(solution)/shard_map/reduce_scatter | solution.py:173
  247.8 7.0 %copy-start.24 = (bf16[256,704]{0,1:T(8,128)(2,1)S(1)}, bf16[256,704]{0,1:T(8,128)(2,1)}, u32[]{:S(2)}) copy-start(bf16[256,704]{0,1:T(8,128)(2,1)} %copy-done.23) | copy-start | bytes 1081348
  247.9 60.2 %reduce-scatter.17.cloned.1.call-start = ((), (), s32[]{:S(2)}) async-start(), calls=%async_computation.19 | async-start | bytes 786432 | tf_op jit(solution)/shard_map/reduce_scatter | solution.py:215
  250.0 75.6 %reduce-scatter.11.cloned.1.call-start = ((), (), s32[]{:S(2)}) async-start(), calls=%async_computation.16 | async-start | bytes 786432 | tf_op jit(solution)/shard_map/reduce_scatter | solution.py:192
  254.8 98.3 %reduce-scatter.23.cloned.1.call-start = ((), (), s32[]{:S(2)}) async-start(), calls=%async_computation.22 | async-start | bytes 2162688 | tf_op jit(solution)/shard_map/reduce_scatter | solution.py:218
  257.8 35.4 %copy-start.4 = (bf16[1,256,1024]{2,1,0:T(8,128)(2,1)S(1)}, bf16[1,256,1024]{2,1,0:T(8,128)(2,1)}, u32[]{:S(2)}) copy-start(bf16[1,256,1024]{2,1,0:T(8,128)(2,1)} %param.14) | copy-start | bytes 1572868
  257.8 122.8 %reduce-scatter.21.cloned.1.call-start = ((), (), s32[]{:S(2)}) async-start(), calls=%async_computation.21 | async-start | bytes 2162688 | tf_op jit(solution)/shard_map/reduce_scatter | solution.py:204
  259.6 36.3 %copy-start.14 = (bf16[1024,256]{1,0:T(8,128)(2,1)S(1)}, bf16[1024,256]{1,0:T(8,128)(2,1)}, u32[]{:S(2)}) copy-start(bf16[1024,256]{1,0:T(8,128)(2,1)} %copy-done.13) | copy-start | bytes 1572868
  259.6 36.3 %copy-start.33 = (bf16[4,64,256]{2,1,0:T(8,128)(2,1)S(1)}, bf16[4,64,256]{2,1,0:T(8,128)(2,1)}, u32[]{:S(2)}) copy-start(bf16[4,64,256]{2,1,0:T(8,128)(2,1)} %copy-done.32) | copy-start | bytes 393220
  259.6 148.5 %reduce-scatter.19.cloned.1.call-start = ((), (), s32[]{:S(2)}) async-start(), calls=%async_computation.20 | async-start | bytes 2162688 | tf_op jit(solution)/shard_map/reduce_scatter | solution.py:201
  261.3 34.9 %copy-start.18 = (bf16[1024,256]{1,0:T(8,128)(2,1)S(1)}, bf16[1024,256]{1,0:T(8,128)(2,1)}, u32[]{:S(2)}) copy-start(bf16[1024,256]{1,0:T(8,128)(2,1)} %copy-done.17) | copy-start | bytes 1572868
  261.3 164.3 %reduce-scatter.13.cloned.1.call-start = ((), (), s32[]{:S(2)}) async-start(), calls=%async_computation.17 | async-start | bytes 786432 | tf_op jit(solution)/shard_map/reduce_scatter | solution.py:195
  294.5 148.4 %reduce-scatter.15.cloned.1.call-start = ((), (), s32[]{:S(2)}) async-start(), calls=%async_computation.18 | async-start | bytes 786432 | tf_op jit(solution)/shard_map/reduce_scatter | solution.py:198
  295.8 186.4 %all-reduce.18.cloned.1.call-start = ((), (), s32[]{:S(2)}) async-start(), calls=%async_computation.15 | async-start | bytes 2097152 | tf_op jit(solution)/shard_map/psum | solution.py:22
  296.6 146.4 %copy-start.50 = (u32[32]{0:T(128)S(1)}, u32[32]{0:T(128)}, u32[]{:S(2)}) copy-start(u32[32]{0:T(128)} %constant.94) | copy-start | bytes 388
  296.6 146.9 %copy-start.49 = (s32[1,256]{1,0:T(1,128)S(1)}, s32[1,256]{1,0:T(1,128)}, u32[]{:S(2)}) copy-start(s32[1,256]{1,0:T(1,128)} %param.17) | copy-start | bytes 3076
  296.6 187.2 %copy-start.46 = (bf16[1024]{0:T(1024)(128)(2,1)S(1)}, bf16[1024]{0:T(1024)(128)(2,1)}, u32[]{:S(2)}) copy-start(bf16[1024]{0:T(1024)(128)(2,1)} %get-tuple-element.56) | copy-start | bytes 6148
  296.6 205.7 %copy-start.42 = (f32[256]{0:T(256)S(1)}, f32[256]{0:T(256)}, u32[]{:S(2)}) copy-start(f32[256]{0:T(256)} %copy-done.41) | copy-start | bytes 3076
  298.0 311.1 %all-reduce.20.cloned.1.call-start = ((), (), s32[]{:S(2)}) async-start(), calls=%async_computation.24 | async-start | bytes 6422528 | tf_op jit(solution)/shard_map/psum | solution.py:223
  609.1 9.7 %copy-start.28 = (bf16[512,704]{0,1:T(8,128)(2,1)S(1)}, bf16[512,704]{0,1:T(8,128)(2,1)}, u32[]{:S(2)}) copy-start(bf16[512,704]{0,1:T(8,128)(2,1)} %get-tuple-element.80) | copy-start | bytes 2162692
  609.1 11.0 %copy-start.27 = (bf16[704,512]{1,0:T(8,128)(2,1)S(1)}, bf16[704,512]{1,0:T(8,128)(2,1)}, u32[]{:S(2)}) copy-start(bf16[704,512]{1,0:T(8,128)(2,1)} %get-tuple-element.81) | copy-start | bytes 2162692
  (21 other events, 63.7 us)
Sparse Core Ops, SparseCore 0:
  32.0 31.0 all-gather.11
  72.2 34.5 all-reduce.11
  155.1 36.2 all-reduce.13
  198.4 36.7 all-reduce.15
  248.0 44.0 reduce-scatter.8
  294.2 13.8 reduce-scatter.16
  310.9 14.6 reduce-scatter.10
  328.4 24.6 reduce-scatter.22
  355.9 24.6 reduce-scatter.20
  383.3 24.6 reduce-scatter.18
  410.9 14.6 reduce-scatter.12
  428.2 14.6 reduce-scatter.14
  445.9 36.3 all-reduce.17
  485.0 124.0 all-reduce.19
Sparse Core Ops, SparseCore 1:
  74.1 23.8 all-gather.5
  99.4 25.5 all-gather.7
  126.4 25.5 all-gather.9
where the time goes:
time: 630 us; the launch traced here: 629 us
  waiting for transfers between devices  443 us (70%)
  blocking collectives  83.5 us (13%)
  matrix products  42 us (7%)
  other arithmetic  36.8 us (6%)
  between operations  17.6 us (3%)
    psum x4, waiting for transfers between devices, head_total(): return lax.psum(partial_sum, 'tp')  120 us
    psum x1, waiting for transfers between devices, shards(): lax.psum(row_query.astype(jnp.bfloat16), 'ctx').astype(jnp.float32)  104 us
    reduce_scatter x1, waiting for transfers between devices, shards(): lax.psum_scatter(pair_terms, 'ctx', scatter_dimension=1, tiled=True)  30.8 us
    dot_general x20, matrix products, contract(): return jnp.einsum(pattern, left, right, preferred_element_type=jnp.float32)  28.2 us
    reduce_scatter x1, waiting for transfers between devices, shards(): lax.psum_scatter(grad_up.astype(jnp.bfloat16), 'fsdp', scatter_dimension=...  27.6 us
    reduce_scatter x1, waiting for transfers between devices, shards(): lax.psum_scatter(grad_down.astype(jnp.bfloat16), 'fsdp', scatter_dimensio...  27.6 us
    reduce_scatter x1, waiting for transfers between devices, shards(): lax.psum_scatter(grad_gate.astype(jnp.bfloat16), 'fsdp', scatter_dimensio...  27.4 us
    all_gather x1, waiting for transfers between devices, shards(): lax.all_gather(down_weight, 'fsdp', axis=1, tiled=True)  24 us
  transfers between devices with their start and end apart: 17, of which 16 were waited for; matrix products, arithmetic and copies ran while one was open for 6% of the time, Pallas kernels for 0%

commit v1 on v0

--- a/solution.py
+++ b/solution.py
@@ -4,6 +4,18 @@
 from jax.sharding import PartitionSpec as P
 
 HEAD_DIM = 64
+
+
+def collect(shard, axis, dim):
+    ways, here = (lax.axis_size(axis), lax.axis_index(axis))
+    grown, reach = (shard, 1)
+    while reach < ways:
+        theirs = lax.ppermute(grown, axis, [(d, d ^ reach) for d in range(ways)])
+        mine_first = jnp.concatenate([grown, theirs], axis=dim)
+        theirs_first = jnp.concatenate([theirs, grown], axis=dim)
+        grown = jnp.where(here & reach == 0, mine_first, theirs_first)
+        reach = 2 * reach
+    return grown
 
 
 def rms_scale(values_in, scales_in):
@@ -52,7 +64,7 @@
         lax.all_gather(key_weight, "fsdp", axis=0, tiled=True),
         lax.all_gather(value_weight, "fsdp", axis=0, tiled=True),
         lax.all_gather(gate_weight, "fsdp", axis=0, tiled=True),
-        lax.all_gather(up_weight, "fsdp", axis=0, tiled=True),
+        collect(up_weight, "fsdp", 0),
     )
     full_out, full_down = (
         lax.all_gather(out_weight, "fsdp", axis=1, tiled=True),

time: 630 us -> 608 us (0.965)
  waiting for transfers between devices: 443 us -> 421 us
    all_gather x1 -> x0, waiting for transfers between devices: 13.5 us -> none  [shards(): lax.all_gather(up_weight, 'fsdp', axis=0, tiled=True)]
    all_gather x1, waiting for transfers between devices: 24 us -> 16 us  [shards(): lax.all_gather(down_weight, 'fsdp', axis=1, tiled=True)]
    reduce_scatter x1, waiting for transfers between devices: 10 us -> 16.9 us  [shards(): lax.psum_scatter(grad_out.astype(jnp.bfloat16), 'fsdp', scatter_dimension...]
    reduce_scatter x1, waiting for transfers between devices: 17.5 us -> 10.6 us  [shards(): lax.psum_scatter(grad_query.astype(jnp.bfloat16), 'fsdp', scatter_dimensi...]
  transfers between devices with their start and end apart: 17 -> 17, of which waited for: 16 -> 15; matrix products, arithmetic and copies ran while one was open for 6% -> 6% of each run, Pallas kernels for 0% -> 0%
where the time goes in v1:
time: 608 us; the launch traced here: 607 us
  waiting for transfers between devices  421 us (69%)
  blocking collectives  83.6 us (14%)
  matrix products  42.2 us (7%)
  other arithmetic  34.4 us (6%)
  between operations  17.4 us (3%)
  local copies, waits for them, and re-layouts  7.01 us (1%)
    psum x4, waiting for transfers between devices, head_total(): return lax.psum(partial_sum, 'tp')  120 us
    psum x1, waiting for transfers between devices, shards(): lax.psum(row_query.astype(jnp.bfloat16), 'ctx').astype(jnp.float32)  104 us
    reduce_scatter x1, waiting for transfers between devices, shards(): lax.psum_scatter(pair_terms, 'ctx', scatter_dimension=1, tiled=True)  31 us
    dot_general x20, matrix products, contract(): return jnp.einsum(pattern, left, right, preferred_element_type=jnp.float32)  29.8 us
    reduce_scatter x1, waiting for transfers between devices, shards(): lax.psum_scatter(grad_up.astype(jnp.bfloat16), 'fsdp', scatter_dimension=...  27.6 us
    reduce_scatter x1, waiting for transfers between devices, shards(): lax.psum_scatter(grad_gate.astype(jnp.bfloat16), 'fsdp', scatter_dimensio...  27.6 us
    reduce_scatter x1, waiting for transfers between devices, shards(): lax.psum_scatter(grad_down.astype(jnp.bfloat16), 'fsdp', scatter_dimensio...  27.4 us
    psum x1, blocking collectives, shards(): counted, squared = lax.psum((jnp.sum(weighting), placed), ('fsdp', 'ctx'))  21.2 us
  transfers between devices with their start and end apart: 17, of which 15 were waited for; matrix products, arithmetic and copies ran while one was open for 6% of the time, Pallas kernels for 0%

profile of v1, /device:TPU:0, one launch (start us, length us, event | category | flops | bytes accessed | tf_op | source)
XLA Modules:
  0.0 607.2 jit_solution(14014140105631144017)
XLA Ops:
  8.1 10.3 %all_gather.27 = bf16[1024,256]{1,0:T(8,128)(2,1)S(1)} all-gather(bf16[512,256]{1,0:T(8,128)(2,1)} %param.22), channel_id=1, replica_groups=mesh['fsdp'=2,'ctx'=4,'tp'=4] {'fsdp'}, dimensions={0}, use_global_device_ids=true | all-gather | bytes 786432 | tf_op jit(solution)/shard_map/all_gather | solution.py:65
  19.9 8.3 %all_gather.26 = bf16[1024,256]{1,0:T(8,128)(2,1)S(1)} all-gather(bf16[512,256]{1,0:T(8,128)(2,1)} %param.21), channel_id=1, replica_groups=mesh['fsdp'=2,'ctx'=4,'tp'=4] {'fsdp'}, dimensions={0}, use_global_device_ids=true | all-gather | bytes 786432 | tf_op jit(solution)/shard_map/all_gather | solution.py:64
  28.2 1.7 convolution_convert_fusion.11
  31.2 11.1 %all_gather.29 = s32[1,1024]{1,0:T(1,128)S(1)} all-gather(s32[1,256]{1,0:T(1,128)S(1)} %copy-done.49), channel_id=1, replica_groups=mesh['fsdp'=2,'ctx'=4,'tp'=4] {'ctx'}, dimensions={1}, use_global_device_ids=true | all-gather | bytes 5120 | tf_op jit(solution)/shard_map/all_gather | solution.py:73
  42.3 8.4 %all_gather.31 = bf16[1024,256]{1,0:T(8,128)(2,1)S(1)} all-gather(bf16[512,256]{1,0:T(8,128)(2,1)S(1)} %copy-done.36), channel_id=1, replica_groups=mesh['fsdp'=2,'ctx'=4,'tp'=4] {'fsdp'}, dimensions={0}, use_global_device_ids=true | all-gather | bytes 786432 | tf_op jit(solution)/shard_map/all_gather | solution.py:63
  50.8 7.0 %all_gather.32 = bf16[256,1024]{1,0:T(8,128)(2,1)S(1)} all-gather(bf16[256,512]{1,0:T(8,128)(2,1)S(1)} %copy-done.37), channel_id=1, replica_groups=mesh['fsdp'=2,'ctx'=4,'tp'=4] {'fsdp'}, dimensions={1}, use_global_device_ids=true | all-gather | bytes 786432 | tf_op jit(solution)/shard_map/all_gather | solution.py:70
  58.6 3.8 all-gather.9.cloned.1.call-done
  65.5 1.5 fusion
  67.0 1.8 fusion.15
  72.2 33.5 %all-reduce.12.cloned.1.call-done = f32[256,1024]{1,0:T(8,128)} async-done(((f32[256,1024]{1,0:T(8,128)}), f32[256,1024]{1,0:T(8,128)}) %all-reduce.12.cloned.1.call-update) | async-done | bytes 1048592 | tf_op jit(solution)/shard_map/psum | solution.py:34
  107.4 2.1 fusion.13
  110.4 3.5 multiply_convert_fusion.3
  113.9 16.0 %all-gather.7.cloned.1.call-done = bf16[704,1024]{1,0:T(8,128)(2,1)} async-done(((bf16[704,512]{1,0:T(8,128)(2,1)}), bf16[704,1024]{1,0:T(8,128)(2,1)}) %all-gather.7.cloned.1.call-update) | async-done | bytes 1441808 | tf_op jit(solution)/shard_map/all_gather | solution.py:71
  129.9 3.0 fusion.62
  133.0 36.4 %all-reduce.14.cloned.1.call-done = f32[256,1024]{1,0:T(8,128)} async-done(((f32[256,1024]{1,0:T(8,128)}), f32[256,1024]{1,0:T(8,128)}) %all-reduce.14.cloned.1.call-update) | async-done | bytes 1048592 | tf_op jit(solution)/shard_map/psum | solution.py:34
  169.4 1.5 multiply_add_fusion
  171.0 2.7 multiply_convert_fusion.2
  174.6 3.0 convolution_add_fusion.2
  178.6 36.0 %all-reduce.16.cloned.1.call-done = f32[256,1024]{1,0:T(8,128)} async-done(((f32[256,1024]{1,0:T(8,128)}), f32[256,1024]{1,0:T(8,128)}) %all-reduce.16.cloned.1.call-update) | async-done | bytes 1048592 | tf_op jit(solution)/shard_map/psum | solution.py:34
  214.5 3.3 multiply_reduce_fusion.1
  219.3 1.5 copy-done.1
  221.0 1.9 multiply_reduce_fusion
  226.2 1.5 maximum_bitcast_fusion
  227.7 1.8 fusion.14
  230.2 2.3 convolution_convert_fusion.6
  232.6 2.0 convolution_convert_fusion.3
  234.7 1.6 convolution_convert_fusion.1
  236.4 2.7 convolution_convert_fusion
  239.2 1.6 convolution_convert_fusion.2
  241.0 31.0 %reduce-scatter.9.cloned.1.call-done = f32[1,256,512]{1,2,0:T(8,128)} async-done(((f32[1,1024,512]{1,2,0:T(8,128)}), f32[1,256,512]{1,2,0:T(8,128)}) %reduce-scatter.9.cloned.1.call-update) | async-done | bytes 524304 | tf_op jit(solution)/shard_map/reduce_scatter | solution.py:185
  277.9 10.6 %reduce-scatter.11.cloned.1.call-done = bf16[512,256]{1,0:T(8,128)(2,1)} async-done(((bf16[1024,256]{1,0:T(8,128)(2,1)}), bf16[512,256]{1,0:T(8,128)(2,1)}) %reduce-scatter.11.cloned.1.call-update) | async-done | bytes 262160 | tf_op jit(solution)/shard_map/reduce_scatter | solution.py:204
  288.4 16.9 %reduce-scatter.17.cloned.1.call-done = bf16[256,512]{1,0:T(8,128)(2,1)} async-done(((bf16[256,1024]{1,0:T(8,128)(2,1)}), bf16[256,512]{1,0:T(8,128)(2,1)}) %reduce-scatter.17.cloned.1.call-update) | async-done | bytes 262160 | tf_op jit(solution)/shard_map/reduce_scatter | solution.py:227
  305.4 27.6 %reduce-scatter.19.cloned.1.call-done = bf16[512,704]{0,1:T(8,128)(2,1)} async-done(((bf16[1024,704]{0,1:T(8,128)(2,1)}), bf16[512,704]{0,1:T(8,128)(2,1)}) %reduce-scatter.19.cloned.1.call-update) | async-done | bytes 720912 | tf_op jit(solution)/shard_map/reduce_scatter | solution.py:213
  332.9 27.6 %reduce-scatter.21.cloned.1.call-done = bf16[512,704]{0,1:T(8,128)(2,1)} async-done(((bf16[1024,704]{0,1:T(8,128)(2,1)}), bf16[512,704]{0,1:T(8,128)(2,1)}) %reduce-scatter.21.cloned.1.call-update) | async-done | bytes 720912 | tf_op jit(solution)/shard_map/reduce_scatter | solution.py:216
  360.5 27.4 %reduce-scatter.23.cloned.1.call-done = bf16[704,512]{1,0:T(8,128)(2,1)} async-done(((bf16[704,1024]{1,0:T(8,128)(2,1)}), bf16[704,512]{1,0:T(8,128)(2,1)}) %reduce-scatter.23.cloned.1.call-update) | async-done | bytes 720912 | tf_op jit(solution)/shard_map/reduce_scatter | solution.py:230
  387.9 17.5 %reduce-scatter.13.cloned.1.call-done = bf16[512,256]{1,0:T(8,128)(2,1)} async-done(((bf16[1024,256]{1,0:T(8,128)(2,1)}), bf16[512,256]{1,0:T(8,128)(2,1)}) %reduce-scatter.13.cloned.1.call-update) | async-done | bytes 262160 | tf_op jit(solution)/shard_map/reduce_scatter | solution.py:207
  405.4 17.3 %reduce-scatter.15.cloned.1.call-done = bf16[512,256]{1,0:T(8,128)(2,1)} async-done(((bf16[1024,256]{1,0:T(8,128)(2,1)}), bf16[512,256]{1,0:T(8,128)(2,1)}) %reduce-scatter.15.cloned.1.call-update) | async-done | bytes 262160 | tf_op jit(solution)/shard_map/reduce_scatter | solution.py:210
  425.3 21.2 %all-reduce.2 = (f32[2]{0:T(128)S(1)}, f32[]{:T(128)}) all-reduce(f32[2]{0:T(128)S(1)} %compare_select_fusion, f32[]{:T(128)} %convert_reduce_fusion), channel_id=1, replica_groups=mesh['fsdp'=2,'ctx'=4,'tp'=4] {'fsdp','ctx'}, use_global_device_ids=true, to_apply=%region_7.8 | all-reduce | flops 3 | bytes 24 | tf_op jit(solution)/shard_map/psum | solution.py:136
  447.6 14.4 %all-reduce.18.cloned.1.call-done = f32[256,1024]{1,0:T(8,128)} async-done(((f32[256,1024]{1,0:T(8,128)}), f32[256,1024]{1,0:T(8,128)}) %all-reduce.18.cloned.1.call-update) | async-done | bytes 1048592 | tf_op jit(solution)/shard_map/psum | solution.py:34
  462.0 1.6 fusion.17
  463.6 4.9 all-reduce.5
  468.7 12.3 %all-reduce.3 = (bf16[512]{0:T(512)(128)(2,1)S(1)}, bf16[512]{0:T(512)(128)(2,1)S(1)}) all-reduce(bf16[512]{0:T(512)(128)(2,1)S(1)} %dynamic-slice.2, bf16[512]{0:T(512)(128)(2,1)S(1)} %dynamic-slice.4), channel_id=1, replica_groups=mesh['fsdp'=2,'ctx'=4,'tp'=4] {'ctx'}, use_global_device_ids=true, to_apply=%region_18.19 | all-reduce | flops 1024 | bytes 4096 | tf_op jit(solution)/shard_map/psum | solution.py:240
  482.1 2.5 fusion.25
  484.6 104.2 %all-reduce.20.cloned.1.call-done = (bf16[512,256]{1,0:T(8,128)(2,1)}, bf16[512,256]{1,0:T(8,128)(2,1)}, bf16[512,256]{1,0:T(8,128)(2,1)}, bf16[256,512]{1,0:T(8...) async-done(((bf16[512,256]{1,0:T(8,128)(2,1)}, bf16[512,256]{1,0:T(8,128)(2,1)}, bf16[512,256]{1,0:T(8,128)(2,1)}, ...) | async-done | bytes 3211280 | tf_op jit(solution)/shard_map/psum | solution.py:235
  588.9 1.9 convert_element_type.237
  590.7 1.8 convert_element_type.239
  592.5 1.8 convert_element_type.241
  594.4 1.8 convert_element_type.243
  (186 shorter events, 33.4 us)
Async XLA Ops:
  8.0 21.9 %copy-start.4 = (bf16[1,256,1024]{2,1,0:T(8,128)(2,1)S(1)}, bf16[1,256,1024]{2,1,0:T(8,128)(2,1)}, u32[]{:S(2)}) copy-start(bf16[1,256,1024]{2,1,0:T(8,128)(2,1)} %param.14) | copy-start | bytes 1572868
  8.0 21.9 %copy-start.39 = (f32[1024]{0:T(1024)S(1)}, f32[1024]{0:T(1024)}, u32[]{:S(2)}) copy-start(f32[1024]{0:T(1024)} %param.19) | copy-start | bytes 12292
  8.0 23.2 %copy-start.49 = (s32[1,256]{1,0:T(1,128)S(1)}, s32[1,256]{1,0:T(1,128)}, u32[]{:S(2)}) copy-start(s32[1,256]{1,0:T(1,128)} %param.18) | copy-start | bytes 3076
  8.0 34.3 %copy-start.36 = (bf16[512,256]{1,0:T(8,128)(2,1)S(1)}, bf16[512,256]{1,0:T(8,128)(2,1)}, u32[]{:S(2)}) copy-start(bf16[512,256]{1,0:T(8,128)(2,1)} %param.20) | copy-start | bytes 786436
  8.1 54.4 %all-gather.9.cloned.1.call-start = ((), (), s32[]{:S(2)}) async-start(), calls=%async_computation.22 | async-start | bytes 1310720 | tf_op jit(solution)/shard_map/all_gather | solution.py:90
  18.4 23.9 %copy-start.17 = (bf16[1024,256]{1,0:T(8,128)(2,1)}, bf16[1024,256]{1,0:T(8,128)(2,1)S(1)}, u32[]{:S(2)}) copy-start(bf16[1024,256]{1,0:T(8,128)(2,1)S(1)} %all_gather.27) | copy-start | bytes 1572868
  18.4 32.3 %copy-start.37 = (bf16[256,512]{1,0:T(8,128)(2,1)S(1)}, bf16[256,512]{1,0:T(8,128)(2,1)}, u32[]{:S(2)}) copy-start(bf16[256,512]{1,0:T(8,128)(2,1)} %param.23) | copy-start | bytes 786436
  19.9 11.4 %copy-start.43 = (f32[256]{0:T(256)}, f32[256]{0:T(256)S(1)}, u32[]{:S(2)}) copy-start(f32[256]{0:T(256)S(1)} %fusion.18) | copy-start | bytes 3076
  19.9 38.2 %copy-start.46 = (f32[256]{0:T(256)}, f32[256]{0:T(256)S(1)}, u32[]{:S(2)}) copy-start(f32[256]{0:T(256)S(1)} %fusion.44) | copy-start | bytes 3076
  31.2 74.6 %all-reduce.12.cloned.1.call-start = ((), (), s32[]{:S(2)}) async-start(), calls=%async_computation.8 | async-start | bytes 2097152 | tf_op jit(solution)/shard_map/psum | solution.py:34
  50.8 7.3 %copy-start.15 = (bf16[1024,256]{1,0:T(8,128)(2,1)}, bf16[1024,256]{1,0:T(8,128)(2,1)S(1)}, u32[]{:S(2)}) copy-start(bf16[1024,256]{1,0:T(8,128)(2,1)S(1)} %all_gather.31) | copy-start | bytes 1572868
  57.8 11.0 %copy-start.9 = (bf16[256,1024]{1,0:T(8,128)(2,1)}, bf16[256,1024]{1,0:T(8,128)(2,1)S(1)}, u32[]{:S(2)}) copy-start(bf16[256,1024]{1,0:T(8,128)(2,1)S(1)} %all_gather.32) | copy-start | bytes 1572868
  70.7 36.5 %copy-start.38 = (f32[1024]{0:T(1024)S(1)}, f32[1024]{0:T(1024)}, u32[]{:S(2)}) copy-start(f32[1024]{0:T(1024)} %param.24) | copy-start | bytes 12292
  70.8 36.7 %all-gather.5.cloned.1.call-start = ((), (), s32[]{:S(2)}) async-start(), calls=%async_computation.9 | async-start | bytes 2162688 | tf_op jit(solution)/shard_map/all_gather | solution.py:66
  71.3 58.6 %all-gather.7.cloned.1.call-start = ((), (), s32[]{:S(2)}) async-start(), calls=%async_computation.10 | async-start | bytes 2162688 | tf_op jit(solution)/shard_map/all_gather | solution.py:71
  71.4 38.2 %collective-permute-start = (bf16[512,704]{0,1:T(8,128)(2,1)S(1)}, bf16[512,704]{0,1:T(8,128)(2,1)}, u32[]{:S(2)}, u32[]{:S(2)}) collective-permute-start(bf16[512,704]{0,1:T(8,128)(2,1)S(1)} %copy-done.52), channel_id=1, source_target_pairs={{0,16},{16,0},{1,17},{17,1},{2,18},{18,2},{3,19},{19,3},{4,20},{20... | collective-permute-start | bytes 2162696 | tf_op jit(solution)/shard_map/ppermute | solution.py:13
  72.2 97.2 %all-reduce.14.cloned.1.call-start = ((), (), s32[]{:S(2)}) async-start(), calls=%async_computation.11 | async-start | bytes 2097152 | tf_op jit(solution)/shard_map/psum | solution.py:34
  107.2 6.7 %copy-start.45 = (f32[256]{0:T(256)}, f32[256]{0:T(256)S(1)}, u32[]{:S(2)}) copy-start(f32[256]{0:T(256)S(1)} %get-tuple-element.84) | copy-start | bytes 3076
  107.4 6.5 %copy-start.6 = (bf16[256,1024]{1,0:T(8,128)(2,1)}, bf16[256,1024]{1,0:T(8,128)(2,1)S(1)}, u32[]{:S(2)}) copy-start(bf16[256,1024]{1,0:T(8,128)(2,1)S(1)} %multiply_convert_fusion.1) | copy-start | bytes 1572868
  113.9 55.5 %copy-start.23 = (bf16[256,704]{0,1:T(8,128)(2,1)}, bf16[256,704]{0,1:T(8,128)(2,1)S(1)}, u32[]{:S(2)}) copy-start(bf16[256,704]{0,1:T(8,128)(2,1)S(1)} %get-tuple-element.93) | copy-start | bytes 1081348
  113.9 19.1 %copy-start.50 = (s32[1,256]{1,0:T(1,128)S(1)}, s32[1,256]{1,0:T(1,128)}, u32[]{:S(2)}) copy-start(s32[1,256]{1,0:T(1,128)} %param.17) | copy-start | bytes 3076
  113.9 55.5 %copy-start.14 = (bf16[1,256,1024]{2,1,0:T(8,128)(2,1)S(1)}, bf16[1,256,1024]{2,1,0:T(8,128)(2,1)}, u32[]{:S(2)}) copy-start(bf16[1,256,1024]{2,1,0:T(8,128)(2,1)} %param.16) | copy-start | bytes 1572868
  129.9 39.5 %copy-start.29 = (bf16[1,256,1024]{2,1,0:T(8,128)(2,1)S(1)}, bf16[1,256,1024]{2,1,0:T(8,128)(2,1)}, u32[]{:S(2)}) copy-start(bf16[1,256,1024]{2,1,0:T(8,128)(2,1)} %param.15) | copy-start | bytes 1572868
  132.9 81.6 %all-reduce.16.cloned.1.call-start = ((), (), s32[]{:S(2)}) async-start(), calls=%async_computation.12 | async-start | bytes 2097152 | tf_op jit(solution)/shard_map/psum | solution.py:34
  133.0 40.7 %copy-start.42 = (f32[1,256]{1,0:T(1,128)}, f32[1,256]{1,0:T(1,128)S(1)}, u32[]{:S(2)}) copy-start(f32[1,256]{1,0:T(1,128)S(1)} %convert_element_type.214) | copy-start | bytes 3076
  171.0 47.7 %copy-start.2 = (f32[256,1024]{1,0:T(8,128)}, f32[256,1024]{1,0:T(8,128)S(1)}, u32[]{:S(2)}) copy-start(f32[256,1024]{1,0:T(8,128)S(1)} %multiply_add_fusion) | copy-start | bytes 3145732
  174.6 40.0 %copy-start.12 = (f32[256,1024]{1,0:T(8,128)S(1)}, f32[256,1024]{1,0:T(8,128)}, u32[]{:S(2)}) copy-start(f32[256,1024]{1,0:T(8,128)} %all-reduce.14.cloned.1.call-done) | copy-start | bytes 3145732
  177.6 94.3 %reduce-scatter.9.cloned.1.call-start = ((), (), s32[]{:S(2)}) async-start(), calls=%async_computation.13 | async-start | bytes 2621440 | tf_op jit(solution)/shard_map/reduce_scatter | solution.py:185
  227.7 7.0 %copy-start.22 = (bf16[256,704]{0,1:T(8,128)(2,1)S(1)}, bf16[256,704]{0,1:T(8,128)(2,1)}, u32[]{:S(2)}) copy-start(bf16[256,704]{0,1:T(8,128)(2,1)} %copy-done.21) | copy-start | bytes 1081348
  227.7 60.8 %reduce-scatter.11.cloned.1.call-start = ((), (), s32[]{:S(2)}) async-start(), calls=%async_computation.15 | async-start | bytes 786432 | tf_op jit(solution)/shard_map/reduce_scatter | solution.py:204
  232.5 72.8 %reduce-scatter.17.cloned.1.call-start = ((), (), s32[]{:S(2)}) async-start(), calls=%async_computation.18 | async-start | bytes 786432 | tf_op jit(solution)/shard_map/reduce_scatter | solution.py:227
  234.6 98.3 %reduce-scatter.19.cloned.1.call-start = ((), (), s32[]{:S(2)}) async-start(), calls=%async_computation.19 | async-start | bytes 2162688 | tf_op jit(solution)/shard_map/reduce_scatter | solution.py:213
  236.4 124.1 %reduce-scatter.21.cloned.1.call-start = ((), (), s32[]{:S(2)}) async-start(), calls=%async_computation.20 | async-start | bytes 2162688 | tf_op jit(solution)/shard_map/reduce_scatter | solution.py:216
  239.2 33.8 %copy-start.5 = (bf16[1,256,1024]{2,1,0:T(8,128)(2,1)S(1)}, bf16[1,256,1024]{2,1,0:T(8,128)(2,1)}, u32[]{:S(2)}) copy-start(bf16[1,256,1024]{2,1,0:T(8,128)(2,1)} %param.14) | copy-start | bytes 1572868
  239.2 148.7 %reduce-scatter.23.cloned.1.call-start = ((), (), s32[]{:S(2)}) async-start(), calls=%async_computation.21 | async-start | bytes 2162688 | tf_op jit(solution)/shard_map/reduce_scatter | solution.py:230
  240.9 34.8 %copy-start.16 = (bf16[1024,256]{1,0:T(8,128)(2,1)S(1)}, bf16[1024,256]{1,0:T(8,128)(2,1)}, u32[]{:S(2)}) copy-start(bf16[1024,256]{1,0:T(8,128)(2,1)} %copy-done.15) | copy-start | bytes 1572868
  240.9 34.8 %copy-start.34 = (bf16[4,64,256]{2,1,0:T(8,128)(2,1)S(1)}, bf16[4,64,256]{2,1,0:T(8,128)(2,1)}, u32[]{:S(2)}) copy-start(bf16[4,64,256]{2,1,0:T(8,128)(2,1)} %copy-done.33) | copy-start | bytes 393220
  240.9 164.5 %reduce-scatter.13.cloned.1.call-start = ((), (), s32[]{:S(2)}) async-start(), calls=%async_computation.16 | async-start | bytes 786432 | tf_op jit(solution)/shard_map/reduce_scatter | solution.py:207
  274.3 148.4 %reduce-scatter.15.cloned.1.call-start = ((), (), s32[]{:S(2)}) async-start(), calls=%async_computation.17 | async-start | bytes 786432 | tf_op jit(solution)/shard_map/reduce_scatter | solution.py:210
  275.6 186.4 %all-reduce.18.cloned.1.call-start = ((), (), s32[]{:S(2)}) async-start(), calls=%async_computation.14 | async-start | bytes 2097152 | tf_op jit(solution)/shard_map/psum | solution.py:34
  276.4 146.3 %copy-start.54 = (u32[32]{0:T(128)S(1)}, u32[32]{0:T(128)}, u32[]{:S(2)}) copy-start(u32[32]{0:T(128)} %constant.97) | copy-start | bytes 388
  276.4 146.9 %copy-start.51 = (s32[1,256]{1,0:T(1,128)S(1)}, s32[1,256]{1,0:T(1,128)}, u32[]{:S(2)}) copy-start(s32[1,256]{1,0:T(1,128)} %param.17) | copy-start | bytes 3076
  277.8 185.8 %copy-start.48 = (bf16[1024]{0:T(1024)(128)(2,1)S(1)}, bf16[1024]{0:T(1024)(128)(2,1)}, u32[]{:S(2)}) copy-start(bf16[1024]{0:T(1024)(128)(2,1)} %get-tuple-element.56) | copy-start | bytes 6148
  277.8 204.3 %copy-start.44 = (f32[256]{0:T(256)S(1)}, f32[256]{0:T(256)}, u32[]{:S(2)}) copy-start(f32[256]{0:T(256)} %copy-done.43) | copy-start | bytes 3076
  277.8 311.1 %all-reduce.20.cloned.1.call-start = ((), (), s32[]{:S(2)}) async-start(), calls=%async_computation.23 | async-start | bytes 6422528 | tf_op jit(solution)/shard_map/psum | solution.py:235
  588.9 7.3 %copy-start.27 = (bf16[512,704]{0,1:T(8,128)(2,1)S(1)}, bf16[512,704]{0,1:T(8,128)(2,1)}, u32[]{:S(2)}) copy-start(bf16[512,704]{0,1:T(8,128)(2,1)} %get-tuple-element.79) | copy-start | bytes 2162692
  588.9 8.6 %copy-start.26 = (bf16[512,704]{0,1:T(8,128)(2,1)S(1)}, bf16[512,704]{0,1:T(8,128)(2,1)}, u32[]{:S(2)}) copy-start(bf16[512,704]{0,1:T(8,128)(2,1)} %get-tuple-element.80) | copy-start | bytes 2162692
  592.5 6.3 %copy-start.25 = (bf16[704,512]{1,0:T(8,128)(2,1)S(1)}, bf16[704,512]{1,0:T(8,128)(2,1)}, u32[]{:S(2)}) copy-start(bf16[704,512]{1,0:T(8,128)(2,1)} %get-tuple-element.81) | copy-start | bytes 2162692
  (25 other events, 56.1 us)
Sparse Core Ops, SparseCore 0:
  31.3 31.0 all-gather.8
  70.9 34.8 all-reduce.11
  133.1 36.2 all-reduce.13
  177.8 36.7 all-reduce.15
  227.8 44.0 reduce-scatter.8
  274.6 13.7 reduce-scatter.10
  290.7 14.6 reduce-scatter.16
  308.2 24.6 reduce-scatter.18
  335.7 24.6 reduce-scatter.20
  363.1 24.6 reduce-scatter.22
  390.7 14.6 reduce-scatter.12
  408.1 14.6 reduce-scatter.14
  425.7 36.2 all-reduce.17
  464.8 124.0 all-reduce.19
Sparse Core Ops, SparseCore 1:
  72.8 31.1 all-gather.4
  105.4 24.5 all-gather.6
